TPU v7x, 128 devices: a whole 4x4x4 slice. The times are simulated.
128 devices in a mesh: grp: 4 (over z), slab: 32 (over y, x, core).
Axes of the slice: x: 4, y: 4, z: 4, core: 2. Of those that a mesh axis runs over, the one named last changes fastest.
Arguments:
- tensor: float32 [672, 256, 672], P('grp', 'slab'), may hold values from -20 to 20
- start_one: float32 [672, 96], replicated, may hold values from -6 to 6
- start_two: float32 [672, 96], replicated, may hold values from -6 to 6
Outputs:
- basis_one: float32 [672, 96], replicated
- basis_two: float32 [672, 96], replicated
- core: float32 [96, 256, 96], P('grp', 'slab')
All inputs are finite; a program needn't handle non-finite values.
Results may differ from a plain program's by a relative error of at most 0.0003.
Values sent between devices are 32-bit elements; how exact they have to be, the bound alone decides.
A program may use at most 64 MiB of HBM per device.

v0:
```python
import jax
import jax.numpy as jnp
from jax import lax
from jax.sharding import PartitionSpec as P

ITERS = 2


HIGH = lax.Precision.HIGHEST


def orthonormal(widened):
    cross = jnp.dot(widened.T, widened, precision=HIGH)
    lower_small = jnp.linalg.cholesky(cross)
    return lax.linalg.triangular_solve(
        lower_small, widened, left_side=False, lower=True, transpose_a=True
    )


def iterate_basis(gram, start):
    current = start
    for _ in range(ITERS):
        current = orthonormal(jnp.dot(gram, current, precision=HIGH))
    return current


def local(tensor, start_one, start_two):
    block_gram = jnp.einsum("jmi,jmk->ik", tensor, tensor, precision=HIGH)
    gram_one = lax.psum(block_gram, ("grp", "slab"))
    basis_one = iterate_basis(gram_one, start_one)
    reduced = jnp.einsum("jmi,ia->jma", tensor, basis_one, precision=HIGH)
    regrouped = lax.all_to_all(reduced, "grp", split_axis=1, concat_axis=0, tiled=True)
    block_second = jnp.einsum("jma,kma->jk", regrouped, regrouped, precision=HIGH)
    gram_two = lax.psum(block_second, ("grp", "slab"))
    basis_two = iterate_basis(gram_two, start_two)
    second_rows = tensor.shape[0]
    own_basis = lax.dynamic_slice_in_dim(
        basis_two, lax.axis_index("grp") * second_rows, second_rows, 0
    )
    partial_core = jnp.einsum("jb,jma->bma", own_basis, reduced, precision=HIGH)
    core = lax.psum_scatter(partial_core, "grp", scatter_dimension=0, tiled=True)
    return (basis_one, basis_two, core)


def solution(mesh):
    in_specs = (P("grp", "slab", None), P(), P())
    out_specs = (P(), P(), P("grp", "slab", None))
    return jax.shard_map(local, mesh=mesh, in_specs=in_specs, out_specs=out_specs, check_vma=False)
```

profile of v0, /device:TPU:0, one launch (start us, length us, event | category | flops | bytes accessed | tf_op | source)
XLA Modules:
  0.0 465.3 jit_solution(15145513758969465968)
XLA Ops:
  7.2 18.1 %fusion.4 = f32[672,672]{1,0:T(8,128)} fusion(f32[168,8,672]{2,1,0:T(8,128)} %param.6), kind=kOutput, calls=%fused_computation.5 | convolution fusion | flops 7283146752 | bytes 5419008 | tf_op jit(solution)/shard_map/jmi,jmk->ik/dot_general | solution.py:28
  25.6 152.5 %all-reduce.3.cloned.1.call-done = f32[672,672]{1,0:T(8,128)} async-done(((f32[672,672]{1,0:T(8,128)}), f32[672,672]{1,0:T(8,128)}) %all-reduce.3.cloned.1.call-update) | async-done | bytes 1806352 | tf_op jit(solution)/shard_map/psum | solution.py:29
  178.1 3.7 fusion.30
  182.3 8.8 %cholesky.74 = f32[96,96]{1,0:T(8,128)S(1)} custom-call(f32[96,96]{1,0:T(8,128)S(1)} %fusion.26), custom_call_target="Cholesky" | custom-call | tf_op jit(solution)/shard_map/jit(cholesky)/cholesky | solution.py:14
  191.1 0.6 compare_reduce_fusion.3
  191.7 0.7 fusion.14
  192.4 7.4 %custom-call.8 = f32[1,96,96]{1,2,0:T(8,128)S(1)} custom-call(f32[1,96,96]{2,1,0:T(8,128)S(1)} %fusion.14), custom_call_target="InvertDiagBlocksLowerTriangular" | custom-call | tf_op jit(solution)/shard_map/triangular_solve/custom-call.0 | solution.py:15
  199.8 0.4 convolution_bitcast_fusion.3
  200.2 2.0 fusion.32
  202.7 8.8 %cholesky.85 = f32[96,96]{1,0:T(8,128)S(1)} custom-call(f32[96,96]{1,0:T(8,128)S(1)} %fusion.24), custom_call_target="Cholesky" | custom-call | tf_op jit(solution)/shard_map/jit(cholesky)/cholesky | solution.py:14
  211.5 0.6 compare_reduce_fusion.2
  212.1 0.7 fusion.15
  212.8 7.4 %custom-call.9 = f32[1,96,96]{1,2,0:T(8,128)S(1)} custom-call(f32[1,96,96]{2,1,0:T(8,128)S(1)} %fusion.15), custom_call_target="InvertDiagBlocksLowerTriangular" | custom-call | tf_op jit(solution)/shard_map/triangular_solve/custom-call.0 | solution.py:15
  220.6 6.5 %fusion.7 = f32[168,8,96]{2,0,1:T(8,128)S(1)} fusion(f32[168,8,672]{2,1,0:T(8,128)} %param.6, f32[96,672]{1,0:T(8,128)S(1)} %fusion.22), kind=kOutput, calls=%fused_computation.6 | convolution fusion | flops 1040449536 | bytes 4386816 | tf_op jit(solution)/shard_map/jmi,ia->jma/dot_general | solution.py:31
  227.1 15.1 %all_to_all.18 = f32[168,8,96]{2,0,1:T(8,128)S(1)} all-to-all(f32[168,8,96]{2,0,1:T(8,128)S(1)} %fusion.7), channel_id=1, replica_groups=mesh['grp'=4,'slab'=32] {'grp'}, dimensions={1} | all-to-all | bytes 1032192 | tf_op jit(solution)/shard_map/all_to_all | solution.py:32
  242.2 3.1 convolution_bitcast_fusion
  245.4 147.7 %all-reduce.5.cloned.1.call-done = f32[672,672]{1,0:T(8,128)} async-done(((f32[672,672]{1,0:T(8,128)}), f32[672,672]{1,0:T(8,128)}) %all-reduce.5.cloned.1.call-update) | async-done | bytes 1806352 | tf_op jit(solution)/shard_map/psum | solution.py:34
  393.1 3.7 fusion.34
  397.3 8.8 %cholesky.96 = f32[96,96]{1,0:T(8,128)S(1)} custom-call(f32[96,96]{1,0:T(8,128)S(1)} %fusion.21), custom_call_target="Cholesky" | custom-call | tf_op jit(solution)/shard_map/jit(cholesky)/cholesky | solution.py:14
  406.1 0.6 compare_reduce_fusion.1
  406.7 0.7 fusion.16
  407.4 7.4 %custom-call.10 = f32[1,96,96]{1,2,0:T(8,128)S(1)} custom-call(f32[1,96,96]{2,1,0:T(8,128)S(1)} %fusion.16), custom_call_target="InvertDiagBlocksLowerTriangular" | custom-call | tf_op jit(solution)/shard_map/triangular_solve/custom-call.0 | solution.py:15
  414.8 0.4 convolution_bitcast_fusion.2
  415.2 2.0 fusion.36
  417.7 8.8 %cholesky.107 = f32[96,96]{1,0:T(8,128)S(1)} custom-call(f32[96,96]{1,0:T(8,128)S(1)} %fusion.19), custom_call_target="Cholesky" | custom-call | tf_op jit(solution)/shard_map/jit(cholesky)/cholesky | solution.py:14
  426.5 0.6 compare_reduce_fusion
  427.2 0.7 fusion.17
  427.8 7.4 %custom-call.11 = f32[1,96,96]{1,2,0:T(8,128)S(1)} custom-call(f32[1,96,96]{2,1,0:T(8,128)S(1)} %fusion.17), custom_call_target="InvertDiagBlocksLowerTriangular" | custom-call | tf_op jit(solution)/shard_map/triangular_solve/custom-call.0 | solution.py:15
  435.2 0.4 convolution_bitcast_fusion.1
  435.7 1.3 fusion.11
  437.0 19.9 %reduce-scatter.2.cloned.1.call-done = f32[24,8,96]{2,0,1:T(8,128)} async-done(((f32[96,8,96]{2,0,1:T(8,128)}), f32[24,8,96]{2,0,1:T(8,128)}) %reduce-scatter.2.cloned.1.call-update) | async-done | bytes 73744 | tf_op jit(solution)/shard_map/reduce_scatter | solution.py:41
  456.8 1.6 copy.27
  (34 shorter events, 2.9 us)
Async XLA Ops:
  7.2 170.9 %copy-start = (f32[672,96]{0,1:T(8,128)S(1)}, f32[672,96]{0,1:T(8,128)}, u32[]{:S(2)}) copy-start(f32[672,96]{0,1:T(8,128)} %param.7) | copy-start | bytes 774148
  7.2 170.9 %all-reduce.3.cloned.1.call-start = ((), (), s32[]{:S(2)}) async-start(), calls=%async_computation.2 | async-start | bytes 4128768 | tf_op jit(solution)/shard_map/psum | solution.py:29
  25.3 367.8 %all-reduce.5.cloned.1.call-start = ((), (), s32[]{:S(2)}) async-start(), calls=%async_computation.3 | async-start | bytes 4128768 | tf_op jit(solution)/shard_map/psum | solution.py:34
  178.1 22.1 %copy-start.2 = (f32[672,672]{1,0:T(8,128)S(1)}, f32[672,672]{1,0:T(8,128)}, u32[]{:S(2)}) copy-start(f32[672,672]{1,0:T(8,128)} %all-reduce.3.cloned.1.call-done) | copy-start | bytes 5419012
  220.6 6.5 %copy-start.3 = (f32[96,672]{1,0:T(8,128)}, f32[96,672]{1,0:T(8,128)S(1)}, u32[]{:S(2)}) copy-start(f32[96,672]{1,0:T(8,128)S(1)} %fusion.22) | copy-start | bytes 774148
  245.3 211.5 %reduce-scatter.2.cloned.1.call-start = ((), (), s32[]{:S(2)}) async-start(), calls=%async_computation.4 | async-start | bytes 491520 | tf_op jit(solution)/shard_map/reduce_scatter | solution.py:41
  393.1 22.1 %copy-start.1 = (f32[672,672]{1,0:T(8,128)S(1)}, f32[672,672]{1,0:T(8,128)}, u32[]{:S(2)}) copy-start(f32[672,672]{1,0:T(8,128)} %all-reduce.5.cloned.1.call-done) | copy-start | bytes 5419012
  435.6 22.8 %copy-start.4 = (f32[672,96]{0,1:T(8,128)}, f32[672,96]{0,1:T(8,128)S(1)}, u32[]{:S(2)}) copy-start(f32[672,96]{0,1:T(8,128)S(1)} %convolution_bitcast_fusion.1) | copy-start | bytes 774148
Sparse Core Ops, SparseCore 0:
  25.5 152.5 all-reduce.2
  245.4 147.5 all-reduce.4
  437.1 19.7 reduce-scatter.1
where the time goes:
time: 471 us; the launch traced here: 465 us
  waiting for transfers between devices  320 us (68%)
  other arithmetic  69.9 us (15%)
  matrix products  43.5 us (9%)
  blocking collectives  15.1 us (3%)
  between operations  14.4 us (3%)
    psum x1, waiting for transfers between devices, local(): gram_one = lax.psum(block_gram, ('grp', 'slab'))  153 us
    psum x1, waiting for transfers between devices, local(): gram_two = lax.psum(block_second, ('grp', 'slab'))  148 us
    another operation x12, other arithmetic, orthonormal(): lower_small = jnp.linalg.cholesky(cross)  37.8 us
    another operation x8, other arithmetic, orthonormal(): lax.linalg.triangular_solve(lower_small, widened, left_side=False, lower=...  32 us
    reduce_scatter x1, waiting for transfers between devices, local(): lax.psum_scatter(partial_core, 'grp', scatter_dimension=0, tiled=True)  19.9 us
    dot_general x1, matrix products, local(): block_gram = jnp.einsum('jmi,jmk->ik', tensor, tensor, precision=HIGH)  18.1 us
    all_to_all x1, blocking collectives, local(): lax.all_to_all(reduced, 'grp', split_axis=1, concat_axis=0, tiled=True)  15.1 us
    dot_general x4, matrix products, iterate_basis(): current = orthonormal(jnp.dot(gram, current, precision=HIGH))  11.3 us
  transfers between devices with their start and end apart: 3, of which 3 were waited for; matrix products, arithmetic and copies ran while one was open for 0% of the time, Pallas kernels for 0%

commit v1 on v0

v1 whole, which is shorter than its diff:
```python
import jax
import jax.numpy as jnp
from jax import lax
from jax.experimental import pallas as pl
from jax.experimental.pallas import tpu as pltpu
from jax.sharding import PartitionSpec as P

MESH = pl.DeviceIdType.MESH
F32 = jnp.float32
BF16 = jnp.bfloat16

N = 672
NP = 768
RANK = 96
LANES = 128
GRP = 4
COLS = 8
ROWS = N // GRP
CHUNK = 448
CHUNKS = ROWS * COLS // CHUNK
CHIPS = 64
FOLD = N // 4
NT = (((0,), (0,)), ((), ()))
NN = (((1,), (0,)), ((), ()))
TN = (((1,), (1,)), ((), ()))


def dot(a, b, dims):
    return lax.dot_general(a, b, dims, preferred_element_type=F32)


def split(x):
    high = x.astype(BF16)
    return high, (x - high.astype(F32)).astype(BF16)


def halves(x):
    return x[:, :LANES] + x[:, LANES:]


def tops(x):
    return x[:LANES] + x[LANES:]


def lane(shape):
    return lax.broadcasted_iota(jnp.int32, shape, len(shape) - 1)


def kernel(
    tensor, start_one, start_two, out_one, out_two, out_core,
    staged, high, low, block, width, rhigh, rlow, rtilde, mode, given,
    packed, summed, pair, gathered, core_out, core_in,
    upper, lower, inverse, stacked,
    load_sem, send_sem, recv_sem, swap_send, swap_recv,
):
    grp = lax.axis_index("grp")
    slab = lax.axis_index("slab")
    core = lax.rem(slab, 2)
    chip = grp * 16 + slab // 2

    def peer(t):
        return (t // 16, lax.rem(t, 16) * 2 + core)

    twin = (grp, slab + 1 - 2 * core)

    def load(c):
        return pltpu.make_async_copy(
            tensor.at[pl.ds(c * CHUNK, CHUNK)], staged.at[c], load_sem.at[c]
        )

    for c in range(CHUNKS):
        load(c).start()

    barrier = pltpu.get_barrier_semaphore()

    def greet(k, carry):
        pl.semaphore_signal(
            barrier, inc=1, device_id=peer(lax.rem(chip + k, CHIPS)), device_id_type=MESH
        )
        return carry

    lax.fori_loop(1, CHIPS, greet, 0)
    pl.semaphore_signal(barrier, inc=1, device_id=twin, device_id_type=MESH)

    def set_block(x, rows):
        h, l = split(x)
        block[0:rows, :LANES] = h
        block[0:rows, LANES:] = l

    def pad_start(ref):
        width[...] = jnp.zeros_like(width)
        width[0:N, 0:RANK] = ref[...]
        set_block(width[...], NP)

    def prepare(c):
        load(c).wait()
        rows = pl.ds(c * CHUNK, CHUNK)
        h, l = split(staged[c, :, 0:640])
        high[rows, 0:640] = h
        low[rows, 0:640] = l
        h, l = split(staged[c, :, 640:N])
        high[rows, 640:N] = h
        low[rows, 640:N] = l

    def project(c):
        rows = pl.ds(c * CHUNK, CHUNK)
        v = block[...]
        return halves(dot(high[rows, :], v, NN) + dot(low[rows, :], v, NN))

    def product_one(first):
        total = None
        for c in range(CHUNKS):
            rows = pl.ds(c * CHUNK, CHUNK)
            if first:
                prepare(c)
            yh, yl = split(project(c))
            y = jnp.concatenate([yh, yl], axis=1)
            part = tops(dot(y, high[rows, :], NT) + dot(y, low[rows, :], NT))
            total = part if total is None else total + part
        width[...] = total.T

    def product_two():
        v = block[0:N, :]
        z = halves(dot(rhigh[...], v, NT) + dot(rlow[...], v, NT))
        zh, zl = split(z)
        zz = jnp.concatenate([zh, zl], axis=1)
        width[0:N, :] = halves(dot(rhigh[...], zz, NN) + dot(rlow[...], zz, NN))

    def pack(r):
        tail = width[3 * FOLD : N, :]
        keep = lane((FOLD, LANES)) < RANK
        tiles = FOLD // 8
        for b in range(3):
            body = width[b * FOLD : (b + 1) * FOLD, :]
            moved = pltpu.roll(tail, RANK - 32 * b, 1)
            packed[r, b * tiles : (b + 1) * tiles] = jnp.where(keep, body, moved).reshape(
                tiles, 8, LANES
            )
        packed[r, 63] = jnp.zeros((8, LANES), F32)

    def unpack(r):
        squares = gathered[r, 0] * gathered[r, 0]
        for t in range(1, CHIPS):
            squares = squares + gathered[r, t] * gathered[r, t]
        scale = lax.rsqrt(jnp.sum(jnp.sum(squares, axis=1, keepdims=True), axis=0, keepdims=True))
        lanes = lane((FOLD, LANES))
        tiles = FOLD // 8
        tail = jnp.zeros((FOLD, LANES), F32)
        for b in range(3):
            x = gathered[r, b * tiles : (b + 1) * tiles].reshape(FOLD, LANES) * scale
            h, l = split(jnp.where(lanes < RANK, x, 0.0))
            block[b * FOLD : (b + 1) * FOLD, :LANES] = h
            block[b * FOLD : (b + 1) * FOLD, LANES:] = l
            moved = pltpu.roll(x, 32 * b + 32, 1)
            tail = jnp.where((lanes >= 32 * b) & (lanes < 32 * b + 32), moved, tail)
        h, l = split(tail)
        block[3 * FOLD : N, :LANES] = h
        block[3 * FOLD : N, LANES:] = l

    def send_tiles(r, k, src, dst, stage):
        t = lax.rem(chip + k, CHIPS)
        return pltpu.make_async_remote_copy(
            src_ref=src.at[r, t if stage == 0 else chip],
            dst_ref=dst.at[r, chip],
            send_sem=send_sem.at[r, stage],
            recv_sem=recv_sem.at[r, stage],
            device_id=peer(t),
            device_id_type=MESH,
        )

    def send_all(r, src, dst, stage):
        def seven(i, carry):
            for u in range(7):
                send_tiles(r, 1 + 7 * i + u, src, dst, stage).start()
            return carry

        lax.fori_loop(0, 9, seven, 0)

    def bytes_of(ref, r, sem):
        part = ref.at[r, pl.ds(0, CHIPS - 1)]
        return pltpu.make_async_copy(part, part, sem)

    def reduce_block(r, first=None, last=None):
        pack(r)
        if r == 0:
            pl.semaphore_wait(barrier, CHIPS)
        send_all(r, packed, summed, 0)
        summed[r, pl.ds(chip, 1)] = packed[r, pl.ds(chip, 1)]
        if first is not None:
            first()
        bytes_of(summed, r, recv_sem.at[r, 0]).wait()
        total = summed[r, 0]
        for t in range(1, CHIPS):
            total = total + summed[r, t]
        pair[r, pl.ds(core, 1)] = total[None]
        twin_copy = pltpu.make_async_remote_copy(
            src_ref=pair.at[r, core],
            dst_ref=pair.at[r, core],
            send_sem=send_sem.at[r, 1],
            recv_sem=recv_sem.at[r, 1],
            device_id=twin,
            device_id_type=MESH,
        )
        twin_copy.start()
        twin_copy.wait()
        gathered[r, pl.ds(chip, 1)] = (pair[r, 0] + pair[r, 1])[None]
        send_all(r, gathered, gathered, 2)
        if last is not None:
            last()
        bytes_of(gathered, r, recv_sem.at[r, 2]).wait()
        bytes_of(packed, r, send_sem.at[r, 0]).wait()
        bytes_of(gathered, r, send_sem.at[r, 2]).wait()
        unpack(r)

    def cross_of():
        v = block[...]
        x = tops(halves(dot(v, v, NT)))
        upper[...] = x[0:RANK, :]
        rows = lax.broadcasted_iota(jnp.int32, (RANK, LANES), 0)
        lower[...] = jnp.where(rows == lane((RANK, LANES)), 1.0, 0.0)

    def panel(p, tiles):
        start = pl.multiple_of(8 * p, 8)
        u = upper[pl.ds(start, 8), :]
        w = lower[pl.ds(start, 8), :]
        sub = lax.broadcasted_iota(jnp.int32, (8, LANES), 0)
        full = (8, LANES)
        cols = [jnp.broadcast_to(u[:, j : j + 1], full) for j in range(8)]
        urow, wrow, inv, elem = [], [], [], {}
        pivots = jnp.ones(full, F32)
        for j in range(8):
            pivot = jnp.broadcast_to(cols[j][j : j + 1, :], full)
            inv.append(1.0 / pivot)
            pivots = jnp.where(sub == j, pivot, pivots)
            factor = jnp.where(sub > j, cols[j] * inv[j], 0.0)
            urow.append(jnp.broadcast_to(u[j : j + 1, :], full))
            wrow.append(jnp.broadcast_to(w[j : j + 1, :], full))
            u = u - factor * urow[j]
            w = w - factor * wrow[j]
            for k in range(j + 1, 8):
                elem[j, k] = jnp.broadcast_to(cols[k][j : j + 1, :], full)
                cols[k] = cols[k] - factor * elem[j, k]
        inverse[pl.ds(start, 8), :] = w * lax.rsqrt(pivots)
        for t in tiles:
            u = upper[8 * t : 8 * t + 8, :]
            w = lower[8 * t : 8 * t + 8, :]
            cols = [jnp.broadcast_to(u[:, j : j + 1], full) for j in range(8)]
            for j in range(8):
                factor = cols[j] * inv[j]
                u = u - factor * urow[j]
                w = w - factor * wrow[j]
                for k in range(j + 1, 8):
                    cols[k] = cols[k] - factor * elem[j, k]
            upper[8 * t : 8 * t + 8, :] = pltpu.roll(u, LANES - 8, 1)
            lower[8 * t : 8 * t + 8, :] = w

    def panels(first, last):
        def step(p, carry):
            panel(p, range(first + 1, 12))
            return carry

        lax.fori_loop(first, last, step, 0)

    def stack():
        h, l = split(inverse[...])
        stacked[:LANES, :] = h
        stacked[LANES:, :] = l

    def factor_start():
        cross_of()
        panels(0, 4)

    def factor_end():
        panels(4, 8)
        panels(8, 12)
        stack()

    def apply(rows):
        f = stacked[...]
        return halves(dot(block[rows, :LANES], f, TN) + dot(block[rows, LANES:], f, TN))

    high[:, 640:NP] = jnp.zeros((high.shape[0], LANES), BF16)
    low[:, 640:NP] = jnp.zeros((low.shape[0], LANES), BF16)
    inverse[...] = jnp.zeros_like(inverse)
    pad_start(start_one)
    product_one(True)
    reduce_block(0)
    product_one(False)
    reduce_block(1, factor_start, factor_end)
    set_block(apply(slice(0, NP)), NP)

    for c in range(CHUNKS):
        rtilde[c * CHUNK : (c + 1) * CHUNK, :] = project(c)
    for m in range(COLS):
        mode[m // 2, m % 2] = rtilde[pl.ds(m, ROWS, stride=COLS), :]

    def swap(src, dst, k, r):
        g = lax.rem(grp + k, GRP)
        return pltpu.make_async_remote_copy(
            src_ref=src.at[g],
            dst_ref=dst.at[grp],
            send_sem=swap_send.at[r],
            recv_sem=swap_recv.at[r],
            device_id=(g, slab),
            device_id_type=MESH,
        )

    for k in (2, 1, 3):
        swap(mode, given, k, 0).start()
    given[pl.ds(grp, 1)] = mode[pl.ds(grp, 1)]
    factor_start()
    factor_end()
    out_one[...] = apply(slice(0, N))[:, :RANK]
    part = given.at[pl.ds(0, GRP - 1)]
    pltpu.make_async_copy(part, part, swap_recv.at[0]).wait()
    part = mode.at[pl.ds(0, GRP - 1)]
    pltpu.make_async_copy(part, part, swap_send.at[0]).wait()
    f = stacked[...]
    for g in range(GRP):
        for m in range(2):
            h, l = split(given[g, m])
            h, l = split(halves(dot(h, f, TN) + dot(l, f, TN)))
            rhigh[g * ROWS : (g + 1) * ROWS, m * LANES : (m + 1) * LANES] = h
            rlow[g * ROWS : (g + 1) * ROWS, m * LANES : (m + 1) * LANES] = l

    pad_start(start_two)
    product_two()
    reduce_block(2)
    product_two()
    reduce_block(3, factor_start, factor_end)
    set_block(apply(slice(0, NP)), NP)
    v = block[0:N, :]
    partial = tops(dot(v, rhigh[...], NT) + dot(v, rlow[...], NT))
    factor_start()
    factor_end()
    out_two[...] = apply(slice(0, N))[:, :RANK]
    whole = jnp.dot(inverse[...], partial, precision=lax.Precision.HIGHEST)
    for g in range(GRP):
        for m in range(2):
            core_out[g, m] = whole[g * 24 : (g + 1) * 24, m * LANES : (m + 1) * LANES]
    for k in (2, 1, 3):
        swap(core_out, core_in, k, 1).start()
    core_in[pl.ds(grp, 1)] = core_out[pl.ds(grp, 1)]
    part = core_in.at[pl.ds(0, GRP - 1)]
    pltpu.make_async_copy(part, part, swap_recv.at[1]).wait()
    part = core_out.at[pl.ds(0, GRP - 1)]
    pltpu.make_async_copy(part, part, swap_send.at[1]).wait()
    for g in range(GRP):
        for m in range(2):
            out_core[pl.ds(2 * g + m, 24, stride=COLS), :] = core_in[g, m][:, :RANK]


def local(tensor, start_one, start_two):
    rows = ROWS * COLS
    vmem = pl.BlockSpec(memory_space=pltpu.VMEM)
    basis_one, basis_two, core = pl.pallas_call(
        kernel,
        out_shape=(
            jax.ShapeDtypeStruct((N, RANK), F32),
            jax.ShapeDtypeStruct((N, RANK), F32),
            jax.ShapeDtypeStruct((RANK // GRP * COLS, RANK), F32),
        ),
        in_specs=[pl.BlockSpec(memory_space=pl.ANY), vmem, vmem],
        out_specs=(vmem, vmem, vmem),
        scratch_shapes=[
            pltpu.VMEM((CHUNKS, CHUNK, N), F32),
            pltpu.VMEM((rows, NP), BF16),
            pltpu.VMEM((rows, NP), BF16),
            pltpu.VMEM((NP, 2 * LANES), BF16),
            pltpu.VMEM((NP, LANES), F32),
            pltpu.VMEM((N, 2 * LANES), BF16),
            pltpu.VMEM((N, 2 * LANES), BF16),
            pltpu.VMEM((rows, LANES), F32),
            pltpu.VMEM((GRP, 2, ROWS, LANES), F32),
            pltpu.VMEM((GRP, 2, ROWS, LANES), F32),
            pltpu.VMEM((4, CHIPS, 8, LANES), F32),
            pltpu.VMEM((4, CHIPS, 8, LANES), F32),
            pltpu.VMEM((4, 2, 8, LANES), F32),
            pltpu.VMEM((4, CHIPS, 8, LANES), F32),
            pltpu.VMEM((GRP, 2, 24, LANES), F32),
            pltpu.VMEM((GRP, 2, 24, LANES), F32),
            pltpu.VMEM((RANK, LANES), F32),
            pltpu.VMEM((RANK, LANES), F32),
            pltpu.VMEM((LANES, LANES), F32),
            pltpu.VMEM((2 * LANES, LANES), BF16),
            pltpu.SemaphoreType.DMA((CHUNKS,)),
            pltpu.SemaphoreType.DMA((4, 3)),
            pltpu.SemaphoreType.DMA((4, 3)),
            pltpu.SemaphoreType.DMA((2,)),
            pltpu.SemaphoreType.DMA((2,)),
        ],
        compiler_params=pltpu.CompilerParams(
            collective_id=0, has_side_effects=True, vmem_limit_bytes=48 << 20
        ),
    )(tensor.reshape(rows, N), start_one, start_two)
    return basis_one, basis_two, core.reshape(RANK // GRP, COLS, RANK)


def solution(mesh):
    in_specs = (P("grp", "slab", None), P(), P())
    out_specs = (P(), P(), P("grp", "slab", None))
    return jax.shard_map(local, mesh=mesh, in_specs=in_specs, out_specs=out_specs, check_vma=False)
```

time: 471 us -> 108 us (0.23); the launches traced: 465 us -> 108 us
  waiting for transfers between devices: 320 us -> 0 us
  Pallas kernels: 0 us -> 100 us
  other arithmetic: 69.9 us -> 0 us
  matrix products: 43.5 us -> 0 us
  blocking collectives: 15.1 us -> 0 us
  between operations: 14.4 us -> 0.65 us
  local copies, waits for them, and re-layouts: 1.95 us -> 6.81 us
    psum x2 -> x0, waiting for transfers between devices: 300 us -> none  [the longest x1 153 us: local(): gram_one = lax.psum(block_gram, ('grp', 'slab'))]
    pallas_call x0 -> x1, Pallas kernels: none -> 100 us  [local(): pl.pallas_call(kernel, out_shape=(jax.ShapeDtypeStruct((N, RANK), F32), j...]
    another operation x20 -> x0, other arithmetic: 69.9 us -> none  [the longest x12 37.8 us: orthonormal(): lower_small = jnp.linalg.cholesky(cross)]
    dot_general x12 -> x0, matrix products: 41.8 us -> none  [the longest x1 18.1 us: local(): block_gram = jnp.einsum('jmi,jmk->ik', tensor, tensor, precision=HIGH)]
    reduce_scatter x1 -> x0, waiting for transfers between devices: 19.9 us -> none  [local(): lax.psum_scatter(partial_core, 'grp', scatter_dimension=0, tiled=True)]
    all_to_all x1 -> x0, blocking collectives: 15.1 us -> none  [local(): lax.all_to_all(reduced, 'grp', split_axis=1, concat_axis=0, tiled=True)]
    unnamed x11 -> x7, local copies, waits for them, and re-layouts: 1.58 us -> 6.81 us
  transfers between devices with their start and end apart: 3 -> 0, of which waited for: 3 -> 0; matrix products, arithmetic and copies ran while one was open for 0% -> 0% of each run, Pallas kernels for 0% -> 0%
where the time goes in v1:
time: 108 us
  Pallas kernels  100 us (93%)
  local copies, waits for them, and re-layouts  6.81 us (6%)
    pallas_call x1, Pallas kernels, local(): pl.pallas_call(kernel, out_shape=(jax.ShapeDtypeStruct((N, RANK), F32), j...  100 us
    unnamed x7, local copies, waits for them, and re-layouts  6.81 us

profile of v1, /device:TPU:0, one launch (start us, length us, event | category | flops | bytes accessed | tf_op | source)
XLA Modules:
  0.0 107.7 jit_solution(5968082439859962709)
XLA Ops:
  0.6 1.1 %copy.6.start_one = f32[672,96]{1,0:T(8,128)S(1)} copy(f32[672,96]{0,1:T(8,128)} %param.4) | data formatting | bytes 516096 | tf_op args[1]
  1.8 1.1 %copy.7.start_two = f32[672,96]{1,0:T(8,128)S(1)} copy(f32[672,96]{0,1:T(8,128)} %param.5) | data formatting | bytes 516096 | tf_op args[2]
  2.9 0.0 copy-start
  2.9 2.2 %copy-done = f32[168,8,672]{2,1,0:T(8,128)S(1)} copy-done((f32[168,8,672]{2,1,0:T(8,128)S(1)}, f32[168,8,672]{2,1,0:T(8,128)}, u32[]{:S(2)}) %copy-start) | copy-done | bytes 3612696
  5.1 100.3 %shard_map.58 = (f32[672,96]{1,0:T(8,128)S(1)}, f32[672,96]{1,0:T(8,128)S(1)}, f32[192,96]{1,0:T(8,128)S(1)}) custom-call(f32[1344,672]{1,0:T(8,128)S(1)} %bitcast.2, f32[672,96]{1,0:T(8,128)S(1)} %copy.6.start_one, f32[672,96]{1,0:T(8,128)S(1)} %copy.7.start_two), custom_call_target="tpu_custom_call" | custom-call | tf_op jit(solution)/shard_map/pallas_call | solution.py:356
  105.3 0.9 copy.8
  106.2 0.9 copy.9
  107.1 0.6 copy.11
Async XLA Ops:
  2.9 2.2 %copy-start = (f32[168,8,672]{2,1,0:T(8,128)S(1)}, f32[168,8,672]{2,1,0:T(8,128)}, u32[]{:S(2)}) copy-start(f32[168,8,672]{2,1,0:T(8,128)} %param.3) | copy-start | bytes 10838020

commit v2 on v1

--- a/solution.py
+++ b/solution.py
@@ -19,7 +19,10 @@
 CHUNK = 448
 CHUNKS = ROWS * COLS // CHUNK
 CHIPS = 64
+BODY, TAIL = 256, 80
 FOLD = N // 4
+OFFSETS = [(z, y, x) for z in range(4) for y in range(4) for x in range(4)]
+FAR_FIRST = sorted(OFFSETS[1:], key=lambda o: -sum(min(d, 4 - d) for d in o))
 NT = (((0,), (0,)), ((), ()))
 NN = (((1,), (0,)), ((), ()))
 TN = (((1,), (1,)), ((), ()))
@@ -48,7 +51,7 @@
 
 def kernel(
     tensor, start_one, start_two, out_one, out_two, out_core,
-    staged, high, low, block, width, rhigh, rlow, rtilde, mode, given,
+    staged, starts, wide, gram, cross_part, ghigh, glow, high, low, block, exact, width, rhigh, rlow, rtilde, line, mode, given,
     packed, summed, pair, gathered, core_out, core_in,
     upper, lower, inverse, stacked,
     load_sem, send_sem, recv_sem, swap_send, swap_recv,
@@ -61,6 +64,9 @@
     def peer(t):
         return (t // 16, lax.rem(t, 16) * 2 + core)
 
+    zs = [grp] + [lax.rem(grp + d, 4) for d in range(1, 4)]
+    ys = [lax.rem(slab // 8 + d, 4) * 4 for d in range(4)]
+    xs = [lax.rem(slab // 2 + d, 4) for d in range(4)]
     twin = (grp, slab + 1 - 2 * core)
 
     def load(c):
@@ -68,8 +74,15 @@
             tensor.at[pl.ds(c * CHUNK, CHUNK)], staged.at[c], load_sem.at[c]
         )
 
+    def load_start(i):
+        return pltpu.make_async_copy(
+            (start_one, start_two)[i], starts.at[i], load_sem.at[CHUNKS + i]
+        )
+
+    load_start(0).start()
     for c in range(CHUNKS):
         load(c).start()
+    load_start(1).start()
 
     barrier = pltpu.get_barrier_semaphore()
 
@@ -83,14 +96,15 @@
     pl.semaphore_signal(barrier, inc=1, device_id=twin, device_id_type=MESH)
 
     def set_block(x, rows):
+        exact[0:rows, :] = x[0:rows]
         h, l = split(x)
         block[0:rows, :LANES] = h
         block[0:rows, LANES:] = l
 
-    def pad_start(ref):
-        width[...] = jnp.zeros_like(width)
-        width[0:N, 0:RANK] = ref[...]
-        set_block(width[...], NP)
+    def pad_start(i):
+        load_start(i).wait()
+        wide[0:RANK, 0:N] = starts[i]
+        set_block(wide[...].T, NP)
 
     def prepare(c):
         load(c).wait()
@@ -107,17 +121,37 @@
         v = block[...]
         return halves(dot(high[rows, :], v, NN) + dot(low[rows, :], v, NN))
 
-    def product_one(first):
+    def product_one():
         total = None
         for c in range(CHUNKS):
             rows = pl.ds(c * CHUNK, CHUNK)
-            if first:
-                prepare(c)
+            prepare(c)
             yh, yl = split(project(c))
             y = jnp.concatenate([yh, yl], axis=1)
             part = tops(dot(y, high[rows, :], NT) + dot(y, low[rows, :], NT))
             total = part if total is None else total + part
         width[...] = total.T
+
+    def gram_high():
+        for i in range(3):
+            a = high[:, i * 256 : (i + 1) * 256]
+            gram[i * 256 : (i + 1) * 256, i * 256 :] = dot(a, high[:, i * 256 :], NT)
+
+    def gram_low():
+        for i in range(3):
+            a = high[:, i * 256 : (i + 1) * 256]
+            cross_part[i * 256 : (i + 1) * 256, :] = dot(a, low[...], NT)
+        for i in range(3):
+            for j in range(i, 3):
+                a, b = slice(i * 256, (i + 1) * 256), slice(j * 256, (j + 1) * 256)
+                x = gram[a, b] + cross_part[a, b] + cross_part[b, a].T
+                ghigh[a, b], glow[a, b] = split(x)
+                if i != j:
+                    ghigh[b, a], glow[b, a] = split(x.T)
+
+    def product_gram():
+        v = block[...]
+        width[...] = halves(dot(ghigh[...], v, NN) + dot(glow[...], v, NN))
 
     def product_two():
         v = block[0:N, :]
@@ -148,33 +182,29 @@
         tail = jnp.zeros((FOLD, LANES), F32)
         for b in range(3):
             x = gathered[r, b * tiles : (b + 1) * tiles].reshape(FOLD, LANES) * scale
-            h, l = split(jnp.where(lanes < RANK, x, 0.0))
+            x0 = jnp.where(lanes < RANK, x, 0.0)
+            exact[b * FOLD : (b + 1) * FOLD, :] = x0
+            h, l = split(x0)
             block[b * FOLD : (b + 1) * FOLD, :LANES] = h
             block[b * FOLD : (b + 1) * FOLD, LANES:] = l
             moved = pltpu.roll(x, 32 * b + 32, 1)
             tail = jnp.where((lanes >= 32 * b) & (lanes < 32 * b + 32), moved, tail)
+        exact[3 * FOLD : N, :] = tail
         h, l = split(tail)
         block[3 * FOLD : N, :LANES] = h
         block[3 * FOLD : N, LANES:] = l
 
-    def send_tiles(r, k, src, dst, stage):
-        t = lax.rem(chip + k, CHIPS)
-        return pltpu.make_async_remote_copy(
-            src_ref=src.at[r, t if stage == 0 else chip],
-            dst_ref=dst.at[r, chip],
-            send_sem=send_sem.at[r, stage],
-            recv_sem=recv_sem.at[r, stage],
-            device_id=peer(t),
-            device_id_type=MESH,
-        )
-
     def send_all(r, src, dst, stage):
-        def seven(i, carry):
-            for u in range(7):
-                send_tiles(r, 1 + 7 * i + u, src, dst, stage).start()
-            return carry
-
-        lax.fori_loop(0, 9, seven, 0)
+        for dz, dy, dx in FAR_FIRST:
+            part = ys[dy] + xs[dx]
+            pltpu.make_async_remote_copy(
+                src_ref=src.at[r, zs[dz] * 16 + part if stage == 0 else chip],
+                dst_ref=dst.at[r, chip],
+                send_sem=send_sem.at[r, stage],
+                recv_sem=recv_sem.at[r, stage],
+                device_id=(zs[dz], part * 2 + core),
+                device_id_type=MESH,
+            ).start()
 
     def bytes_of(ref, r, sem):
         part = ref.at[r, pl.ds(0, CHIPS - 1)]
@@ -213,8 +243,8 @@
         unpack(r)
 
     def cross_of():
-        v = block[...]
-        x = tops(halves(dot(v, v, NT)))
+        v = exact[0:N, :]
+        x = lax.dot_general(v, v, NT, precision=lax.Precision.HIGHEST, preferred_element_type=F32)
         upper[...] = x[0:RANK, :]
         rows = lax.broadcasted_iota(jnp.int32, (RANK, LANES), 0)
         lower[...] = jnp.where(rows == lane((RANK, LANES)), 1.0, 0.0)
@@ -275,24 +305,37 @@
         panels(8, 12)
         stack()
 
+    def basis():
+        return lax.dot_general(
+            inverse[0:RANK, :], exact[0:N, :], TN,
+            precision=lax.Precision.HIGHEST, preferred_element_type=F32,
+        )
+
     def apply(rows):
-        f = stacked[...]
-        return halves(dot(block[rows, :LANES], f, TN) + dot(block[rows, LANES:], f, TN))
+        return lax.dot_general(exact[rows, :], inverse[...], TN, precision=lax.Precision.HIGHEST, preferred_element_type=F32)
 
     high[:, 640:NP] = jnp.zeros((high.shape[0], LANES), BF16)
     low[:, 640:NP] = jnp.zeros((low.shape[0], LANES), BF16)
     inverse[...] = jnp.zeros_like(inverse)
-    pad_start(start_one)
-    product_one(True)
-    reduce_block(0)
-    product_one(False)
+    wide[...] = jnp.zeros_like(wide)
+    pad_start(0)
+    product_one()
+    reduce_block(0, gram_high, gram_low)
+    product_gram()
     reduce_block(1, factor_start, factor_end)
     set_block(apply(slice(0, NP)), NP)
 
     for c in range(CHUNKS):
         rtilde[c * CHUNK : (c + 1) * CHUNK, :] = project(c)
-    for m in range(COLS):
-        mode[m // 2, m % 2] = rtilde[pl.ds(m, ROWS, stride=COLS), :]
+    keep = lane((TAIL, LANES)) < RANK
+    for g in range(GRP):
+        line[0:ROWS, :] = rtilde[pl.ds(2 * g, ROWS, stride=COLS), :]
+        line[ROWS:, :] = rtilde[pl.ds(2 * g + 1, ROWS, stride=COLS), :]
+        tail = line[BODY:, :]
+        for b in range(3):
+            rows = slice(b * TAIL, (b + 1) * TAIL)
+            mode[g, rows] = jnp.where(keep, line[rows, :], pltpu.roll(tail, RANK - 32 * b, 1))
+        mode[g, 3 * TAIL : BODY] = line[3 * TAIL : BODY, :]
 
     def swap(src, dst, k, r):
         g = lax.rem(grp + k, GRP)
@@ -310,20 +353,31 @@
     given[pl.ds(grp, 1)] = mode[pl.ds(grp, 1)]
     factor_start()
     factor_end()
-    out_one[...] = apply(slice(0, N))[:, :RANK]
+    out_one[...] = basis()
     part = given.at[pl.ds(0, GRP - 1)]
     pltpu.make_async_copy(part, part, swap_recv.at[0]).wait()
     part = mode.at[pl.ds(0, GRP - 1)]
     pltpu.make_async_copy(part, part, swap_send.at[0]).wait()
     f = stacked[...]
+    lanes = lane((TAIL, LANES))
     for g in range(GRP):
+        tail = jnp.zeros((TAIL, LANES), F32)
+        for b in range(3):
+            x = given[g, b * TAIL : (b + 1) * TAIL]
+            line[b * TAIL : (b + 1) * TAIL, :] = jnp.where(lanes < RANK, x, 0.0)
+            inside = (lanes >= 32 * b) & (lanes < 32 * b + 32)
+            tail = jnp.where(inside, pltpu.roll(x, 32 * b + 32, 1), tail)
+        line[3 * TAIL : BODY, :] = given[g, 3 * TAIL : BODY]
+        line[BODY:, :] = tail
+        h, l = split(line[...])
+        y = halves(dot(h, f, TN) + dot(l, f, TN))
         for m in range(2):
-            h, l = split(given[g, m])
-            h, l = split(halves(dot(h, f, TN) + dot(l, f, TN)))
+            h, l = split(y[m * ROWS : (m + 1) * ROWS])
             rhigh[g * ROWS : (g + 1) * ROWS, m * LANES : (m + 1) * LANES] = h
             rlow[g * ROWS : (g + 1) * ROWS, m * LANES : (m + 1) * LANES] = l
 
-    pad_start(start_two)
+    width[N:NP, :] = jnp.zeros((NP - N, LANES), F32)
+    pad_start(1)
     product_two()
     reduce_block(2)
     product_two()
@@ -333,7 +387,7 @@
     partial = tops(dot(v, rhigh[...], NT) + dot(v, rlow[...], NT))
     factor_start()
     factor_end()
-    out_two[...] = apply(slice(0, N))[:, :RANK]
+    out_two[...] = basis()
     whole = jnp.dot(inverse[...], partial, precision=lax.Precision.HIGHEST)
     for g in range(GRP):
         for m in range(2):
@@ -353,26 +407,35 @@
 def local(tensor, start_one, start_two):
     rows = ROWS * COLS
     vmem = pl.BlockSpec(memory_space=pltpu.VMEM)
+    hbm = pl.BlockSpec(memory_space=pltpu.HBM)
     basis_one, basis_two, core = pl.pallas_call(
         kernel,
         out_shape=(
-            jax.ShapeDtypeStruct((N, RANK), F32),
-            jax.ShapeDtypeStruct((N, RANK), F32),
+            jax.ShapeDtypeStruct((RANK, N), F32),
+            jax.ShapeDtypeStruct((RANK, N), F32),
             jax.ShapeDtypeStruct((RANK // GRP * COLS, RANK), F32),
         ),
-        in_specs=[pl.BlockSpec(memory_space=pl.ANY), vmem, vmem],
+        in_specs=[hbm, hbm, hbm],
         out_specs=(vmem, vmem, vmem),
         scratch_shapes=[
             pltpu.VMEM((CHUNKS, CHUNK, N), F32),
+            pltpu.VMEM((2, RANK, N), F32),
+            pltpu.VMEM((LANES, NP), F32),
+            pltpu.VMEM((NP, NP), F32),
+            pltpu.VMEM((NP, NP), F32),
+            pltpu.VMEM((NP, NP), BF16),
+            pltpu.VMEM((NP, NP), BF16),
             pltpu.VMEM((rows, NP), BF16),
             pltpu.VMEM((rows, NP), BF16),
             pltpu.VMEM((NP, 2 * LANES), BF16),
             pltpu.VMEM((NP, LANES), F32),
+            pltpu.VMEM((NP, LANES), F32),
             pltpu.VMEM((N, 2 * LANES), BF16),
             pltpu.VMEM((N, 2 * LANES), BF16),
             pltpu.VMEM((rows, LANES), F32),
-            pltpu.VMEM((GRP, 2, ROWS, LANES), F32),
-            pltpu.VMEM((GRP, 2, ROWS, LANES), F32),
+            pltpu.VMEM((2 * ROWS, LANES), F32),
+            pltpu.VMEM((GRP, BODY, LANES), F32),
+            pltpu.VMEM((GRP, BODY, LANES), F32),
             pltpu.VMEM((4, CHIPS, 8, LANES), F32),
             pltpu.VMEM((4, CHIPS, 8, LANES), F32),
             pltpu.VMEM((4, 2, 8, LANES), F32),
@@ -383,7 +446,7 @@
             pltpu.VMEM((RANK, LANES), F32),
             pltpu.VMEM((LANES, LANES), F32),
             pltpu.VMEM((2 * LANES, LANES), BF16),
-            pltpu.SemaphoreType.DMA((CHUNKS,)),
+            pltpu.SemaphoreType.DMA((CHUNKS + 2,)),
             pltpu.SemaphoreType.DMA((4, 3)),
             pltpu.SemaphoreType.DMA((4, 3)),
             pltpu.SemaphoreType.DMA((2,)),
@@ -392,8 +455,12 @@
         compiler_params=pltpu.CompilerParams(
             collective_id=0, has_side_effects=True, vmem_limit_bytes=48 << 20
         ),
-    )(tensor.reshape(rows, N), start_one, start_two)
-    return basis_one, basis_two, core.reshape(RANK // GRP, COLS, RANK)
+    )(
+        pltpu.with_memory_space_constraint(tensor.reshape(rows, N), pltpu.HBM),
+        pltpu.with_memory_space_constraint(start_one.T, pltpu.HBM),
+        pltpu.with_memory_space_constraint(start_two.T, pltpu.HBM),
+    )
+    return basis_one.T, basis_two.T, core.reshape(RANK // GRP, COLS, RANK)
 
 
 def solution(mesh):

time: 108 us -> 96.9 us (0.90)
  Pallas kernels: 100 us -> 94.1 us
  local copies, waits for them, and re-layouts: 6.81 us -> 2.07 us
    pallas_call x1, Pallas kernels: 100 us -> 94.1 us  [local(): pl.pallas_call(kernel, out_shape=(jax.ShapeDtypeStruct((RANK, N), F32), j...]
    unnamed x7 -> x3, local copies, waits for them, and re-layouts: 6.81 us -> 2.07 us
where the time goes in v2:
time: 96.9 us; the launch traced here: 96.8 us
  Pallas kernels  94.1 us (97%)
  local copies, waits for them, and re-layouts  2.07 us (2%)
    pallas_call x1, Pallas kernels, local(): pl.pallas_call(kernel, out_shape=(jax.ShapeDtypeStruct((RANK, N), F32), j...  94.1 us
    unnamed x3, local copies, waits for them, and re-layouts  2.07 us

profile of v2, /device:TPU:0, one launch (start us, length us, event | category | flops | bytes accessed | tf_op | source)
XLA Modules:
  0.0 96.8 jit_solution(15257552089797850141)
XLA Ops:
  0.6 94.1 %shard_map.58 = (f32[96,672]{1,0:T(8,128)S(1)}, f32[96,672]{1,0:T(8,128)S(1)}, f32[192,96]{1,0:T(8,128)S(1)}) custom-call(f32[1344,672]{1,0:T(8,128)} %bitcast.9, f32[96,672]{1,0:T(8,128)} %bitcast.10, f32[96,672]{1,0:T(8,128)} %bitcast.11), custom_call_target="tpu_custom_call" | custom-call | tf_op jit(solution)/shard_map/pallas_call | solution.py:411
  94.7 0.7 copy.9
  95.4 0.7 copy.10
  96.1 0.6 copy.11

commit v3 on v2

--- a/solution.py
+++ b/solution.py
@@ -19,7 +19,9 @@
 CHUNK = 448
 CHUNKS = ROWS * COLS // CHUNK
 CHIPS = 64
-BODY, TAIL = 256, 80
+STEP = CHUNK // COLS
+BODY, TAIL = 88, 24
+CORE_BODY, CORE_TAIL = 144, 48
 FOLD = N // 4
 OFFSETS = [(z, y, x) for z in range(4) for y in range(4) for x in range(4)]
 FAR_FIRST = sorted(OFFSETS[1:], key=lambda o: -sum(min(d, 4 - d) for d in o))
@@ -53,7 +55,7 @@
     tensor, start_one, start_two, out_one, out_two, out_core,
     staged, starts, wide, gram, cross_part, ghigh, glow, high, low, block, exact, width, rhigh, rlow, rtilde, line, mode, given,
     packed, summed, pair, gathered, core_out, core_in,
-    upper, lower, inverse, stacked,
+    unit, upper, lower, inverse, stacked,
     load_sem, send_sem, recv_sem, swap_send, swap_recv,
 ):
     grp = lax.axis_index("grp")
@@ -79,11 +81,6 @@
             (start_one, start_two)[i], starts.at[i], load_sem.at[CHUNKS + i]
         )
 
-    load_start(0).start()
-    for c in range(CHUNKS):
-        load(c).start()
-    load_start(1).start()
-
     barrier = pltpu.get_barrier_semaphore()
 
     def greet(k, carry):
@@ -95,6 +92,11 @@
     lax.fori_loop(1, CHIPS, greet, 0)
     pl.semaphore_signal(barrier, inc=1, device_id=twin, device_id_type=MESH)
 
+    load_start(0).start()
+    for c in range(CHUNKS):
+        load(c).start()
+    load_start(1).start()
+
     def set_block(x, rows):
         exact[0:rows, :] = x[0:rows]
         h, l = split(x)
@@ -109,10 +111,16 @@
     def prepare(c):
         load(c).wait()
         rows = pl.ds(c * CHUNK, CHUNK)
-        h, l = split(staged[c, :, 0:640])
+        x = staged[c, :, 0:640]
+        squares = jnp.sum((x * x).reshape(CHUNK // 8, 8, 640), axis=0)
+        for k in range(5):
+            packed[0, 63] += squares[:, k * LANES : (k + 1) * LANES]
+        h, l = split(x)
         high[rows, 0:640] = h
         low[rows, 0:640] = l
-        h, l = split(staged[c, :, 640:N])
+        x = staged[c, :, 640:N]
+        packed[0, 63, :, 0 : N - 640] += jnp.sum((x * x).reshape(CHUNK // 8, 8, N - 640), axis=0)
+        h, l = split(x)
         high[rows, 640:N] = h
         low[rows, 640:N] = l
 
@@ -170,13 +178,13 @@
             packed[r, b * tiles : (b + 1) * tiles] = jnp.where(keep, body, moved).reshape(
                 tiles, 8, LANES
             )
-        packed[r, 63] = jnp.zeros((8, LANES), F32)
 
     def unpack(r):
-        squares = gathered[r, 0] * gathered[r, 0]
-        for t in range(1, CHIPS):
-            squares = squares + gathered[r, t] * gathered[r, t]
-        scale = lax.rsqrt(jnp.sum(jnp.sum(squares, axis=1, keepdims=True), axis=0, keepdims=True))
+        if r == 0:
+            squares = gathered[0, 63]
+            trace = jnp.sum(jnp.sum(squares, axis=1, keepdims=True), axis=0, keepdims=True)
+            unit[...] = jnp.broadcast_to(1.0 / trace, (8, LANES))
+        scale = unit[0:1, :]
         lanes = lane((FOLD, LANES))
         tiles = FOLD // 8
         tail = jnp.zeros((FOLD, LANES), F32)
@@ -314,6 +322,7 @@
     def apply(rows):
         return lax.dot_general(exact[rows, :], inverse[...], TN, precision=lax.Precision.HIGHEST, preferred_element_type=F32)
 
+    packed[:, 63] = jnp.zeros((4, 8, LANES), F32)
     high[:, 640:NP] = jnp.zeros((high.shape[0], LANES), BF16)
     low[:, 640:NP] = jnp.zeros((low.shape[0], LANES), BF16)
     inverse[...] = jnp.zeros_like(inverse)
@@ -323,85 +332,113 @@
     reduce_block(0, gram_high, gram_low)
     product_gram()
     reduce_block(1, factor_start, factor_end)
-    set_block(apply(slice(0, NP)), NP)
-
-    for c in range(CHUNKS):
-        rtilde[c * CHUNK : (c + 1) * CHUNK, :] = project(c)
-    keep = lane((TAIL, LANES)) < RANK
-    for g in range(GRP):
-        line[0:ROWS, :] = rtilde[pl.ds(2 * g, ROWS, stride=COLS), :]
-        line[ROWS:, :] = rtilde[pl.ds(2 * g + 1, ROWS, stride=COLS), :]
-        tail = line[BODY:, :]
+    set_block(apply(slice(0, N)), N)
+
+    def fold(target, body, tail):
+        keep = lane((tail, LANES)) < RANK
+        end = line[body : body + tail, :]
         for b in range(3):
-            rows = slice(b * TAIL, (b + 1) * TAIL)
-            mode[g, rows] = jnp.where(keep, line[rows, :], pltpu.roll(tail, RANK - 32 * b, 1))
-        mode[g, 3 * TAIL : BODY] = line[3 * TAIL : BODY, :]
+            rows = slice(b * tail, (b + 1) * tail)
+            target[rows] = jnp.where(keep, line[rows, :], pltpu.roll(end, RANK - 32 * b, 1))
+        if body > 3 * tail:
+            target[3 * tail : body] = line[3 * tail : body, :]
+
+    def unfold(source, start, body, tail):
+        lanes = lane((tail, LANES))
+        end = jnp.zeros((tail, LANES), F32)
+        for b in range(3):
+            x = source[b * tail : (b + 1) * tail]
+            line[start + b * tail : start + (b + 1) * tail, :] = jnp.where(lanes < RANK, x, 0.0)
+            inside = (lanes >= 32 * b) & (lanes < 32 * b + 32)
+            end = jnp.where(inside, pltpu.roll(x, 32 * b + 32, 1), end)
+        if body > 3 * tail:
+            line[start + 3 * tail : start + body, :] = source[3 * tail : body]
+        line[start + body : start + body + tail, :] = end
 
     def swap(src, dst, k, r):
         g = lax.rem(grp + k, GRP)
         return pltpu.make_async_remote_copy(
-            src_ref=src.at[g],
-            dst_ref=dst.at[grp],
+            src_ref=src(g),
+            dst_ref=dst,
             send_sem=swap_send.at[r],
             recv_sem=swap_recv.at[r],
             device_id=(g, slab),
             device_id_type=MESH,
         )
 
-    for k in (2, 1, 3):
-        swap(mode, given, k, 0).start()
-    given[pl.ds(grp, 1)] = mode[pl.ds(grp, 1)]
+    def three(ref, sem):
+        part = ref.at[pl.ds(0, GRP - 1)]
+        return pltpu.make_async_copy(part, part, sem)
+
+    for c in range(CHUNKS):
+        rtilde[c * CHUNK : (c + 1) * CHUNK, :] = project(c)
+        for g in range(GRP):
+            for m in range(2):
+                line[m * STEP : (m + 1) * STEP, :] = rtilde[
+                    pl.ds(c * CHUNK + 2 * g + m, STEP, stride=COLS), :
+                ]
+            fold(mode.at[c, g], BODY, TAIL)
+        for k in (2, 1, 3):
+            swap(lambda g: mode.at[c, g], given.at[c, grp], k, c).start()
+        given[c, pl.ds(grp, 1)] = mode[c, pl.ds(grp, 1)]
     factor_start()
     factor_end()
     out_one[...] = basis()
-    part = given.at[pl.ds(0, GRP - 1)]
-    pltpu.make_async_copy(part, part, swap_recv.at[0]).wait()
-    part = mode.at[pl.ds(0, GRP - 1)]
-    pltpu.make_async_copy(part, part, swap_send.at[0]).wait()
+    width[N:NP, :] = jnp.zeros((NP - N, LANES), F32)
+    pad_start(1)
     f = stacked[...]
-    lanes = lane((TAIL, LANES))
-    for g in range(GRP):
-        tail = jnp.zeros((TAIL, LANES), F32)
-        for b in range(3):
-            x = given[g, b * TAIL : (b + 1) * TAIL]
-            line[b * TAIL : (b + 1) * TAIL, :] = jnp.where(lanes < RANK, x, 0.0)
-            inside = (lanes >= 32 * b) & (lanes < 32 * b + 32)
-            tail = jnp.where(inside, pltpu.roll(x, 32 * b + 32, 1), tail)
-        line[3 * TAIL : BODY, :] = given[g, 3 * TAIL : BODY]
-        line[BODY:, :] = tail
+    for c in range(CHUNKS):
+        three(given.at[c], swap_recv.at[c]).wait()
+        size = 2 * STEP
+        for g in range(GRP):
+            unfold(given.at[c, g], g * size, BODY, TAIL)
         h, l = split(line[...])
         y = halves(dot(h, f, TN) + dot(l, f, TN))
-        for m in range(2):
-            h, l = split(y[m * ROWS : (m + 1) * ROWS])
-            rhigh[g * ROWS : (g + 1) * ROWS, m * LANES : (m + 1) * LANES] = h
-            rlow[g * ROWS : (g + 1) * ROWS, m * LANES : (m + 1) * LANES] = l
-
-    width[N:NP, :] = jnp.zeros((NP - N, LANES), F32)
-    pad_start(1)
+        for g in range(GRP):
+            rows = slice(g * ROWS + c * STEP, g * ROWS + (c + 1) * STEP)
+            for m in range(2):
+                h, l = split(y[g * size + m * STEP : g * size + (m + 1) * STEP])
+                rhigh[rows, m * LANES : (m + 1) * LANES] = h
+                rlow[rows, m * LANES : (m + 1) * LANES] = l
+    for c in range(CHUNKS):
+        three(mode.at[c], swap_send.at[c]).wait()
+
     product_two()
     reduce_block(2)
     product_two()
     reduce_block(3, factor_start, factor_end)
-    set_block(apply(slice(0, NP)), NP)
+    set_block(apply(slice(0, N)), N)
     v = block[0:N, :]
     partial = tops(dot(v, rhigh[...], NT) + dot(v, rlow[...], NT))
+    for m in range(2):
+        line[m * RANK : (m + 1) * RANK, :] = partial[0:RANK, m * LANES : (m + 1) * LANES]
+    fold(core_out, CORE_BODY, CORE_TAIL)
+    for k in (2, 1, 3):
+        swap(lambda g: core_out, core_in.at[grp], k, CHUNKS).start()
+    core_in[pl.ds(grp, 1)] = core_out[...][None]
     factor_start()
     factor_end()
     out_two[...] = basis()
-    whole = jnp.dot(inverse[...], partial, precision=lax.Precision.HIGHEST)
+    mine = inverse[pl.ds(pl.multiple_of(grp * 24, 8), 24), 0:RANK]
+    three(core_in, swap_recv.at[CHUNKS]).wait()
     for g in range(GRP):
+        unfold(core_in.at[g], 0, CORE_BODY, CORE_TAIL)
         for m in range(2):
-            core_out[g, m] = whole[g * 24 : (g + 1) * 24, m * LANES : (m + 1) * LANES]
-    for k in (2, 1, 3):
-        swap(core_out, core_in, k, 1).start()
-    core_in[pl.ds(grp, 1)] = core_out[pl.ds(grp, 1)]
-    part = core_in.at[pl.ds(0, GRP - 1)]
-    pltpu.make_async_copy(part, part, swap_recv.at[1]).wait()
-    part = core_out.at[pl.ds(0, GRP - 1)]
-    pltpu.make_async_copy(part, part, swap_send.at[1]).wait()
-    for g in range(GRP):
-        for m in range(2):
-            out_core[pl.ds(2 * g + m, 24, stride=COLS), :] = core_in[g, m][:, :RANK]
+            x = line[m * RANK : (m + 1) * RANK, :]
+            out_core[pl.ds(2 * g + m, 24, stride=COLS), :] = jnp.dot(
+                mine, x, precision=lax.Precision.HIGHEST
+            )[:, :RANK]
+    for k in range(1, GRP):
+        pltpu.make_async_copy(core_out, core_out, swap_send.at[CHUNKS]).wait()
+
+
+def finish(one, two, core, out_one, out_two, out_core, sems):
+    pairs = ((one, out_one), (two, out_two), (core, out_core))
+    copies = [pltpu.make_async_copy(a, b, sems.at[i]) for i, (a, b) in enumerate(pairs)]
+    for copy in copies:
+        copy.start()
+    for copy in copies:
+        copy.wait()
 
 
 def local(tensor, start_one, start_two):
@@ -433,15 +470,16 @@
             pltpu.VMEM((N, 2 * LANES), BF16),
             pltpu.VMEM((N, 2 * LANES), BF16),
             pltpu.VMEM((rows, LANES), F32),
-            pltpu.VMEM((2 * ROWS, LANES), F32),
-            pltpu.VMEM((GRP, BODY, LANES), F32),
-            pltpu.VMEM((GRP, BODY, LANES), F32),
+            pltpu.VMEM((CHUNK, LANES), F32),
+            pltpu.VMEM((CHUNKS, GRP, BODY, LANES), F32),
+            pltpu.VMEM((CHUNKS, GRP, BODY, LANES), F32),
             pltpu.VMEM((4, CHIPS, 8, LANES), F32),
             pltpu.VMEM((4, CHIPS, 8, LANES), F32),
             pltpu.VMEM((4, 2, 8, LANES), F32),
             pltpu.VMEM((4, CHIPS, 8, LANES), F32),
-            pltpu.VMEM((GRP, 2, 24, LANES), F32),
-            pltpu.VMEM((GRP, 2, 24, LANES), F32),
+            pltpu.VMEM((CORE_BODY, LANES), F32),
+            pltpu.VMEM((GRP, CORE_BODY, LANES), F32),
+            pltpu.VMEM((8, LANES), F32),
             pltpu.VMEM((RANK, LANES), F32),
             pltpu.VMEM((RANK, LANES), F32),
             pltpu.VMEM((LANES, LANES), F32),
@@ -449,8 +487,8 @@
             pltpu.SemaphoreType.DMA((CHUNKS + 2,)),
             pltpu.SemaphoreType.DMA((4, 3)),
             pltpu.SemaphoreType.DMA((4, 3)),
-            pltpu.SemaphoreType.DMA((2,)),
-            pltpu.SemaphoreType.DMA((2,)),
+            pltpu.SemaphoreType.DMA((CHUNKS + 1,)),
+            pltpu.SemaphoreType.DMA((CHUNKS + 1,)),
         ],
         compiler_params=pltpu.CompilerParams(
             collective_id=0, has_side_effects=True, vmem_limit_bytes=48 << 20
@@ -460,6 +498,17 @@
         pltpu.with_memory_space_constraint(start_one.T, pltpu.HBM),
         pltpu.with_memory_space_constraint(start_two.T, pltpu.HBM),
     )
+    basis_one, basis_two, core = pl.pallas_call(
+        finish,
+        out_shape=(
+            jax.ShapeDtypeStruct((RANK, N), F32),
+            jax.ShapeDtypeStruct((RANK, N), F32),
+            jax.ShapeDtypeStruct((RANK // GRP * COLS, RANK), F32),
+        ),
+        in_specs=[vmem, vmem, vmem],
+        out_specs=(hbm, hbm, hbm),
+        scratch_shapes=[pltpu.SemaphoreType.DMA((3,))],
+    )(*(pltpu.with_memory_space_constraint(x, pltpu.VMEM) for x in (basis_one, basis_two, core)))
     return basis_one.T, basis_two.T, core.reshape(RANK // GRP, COLS, RANK)
 
 

time: 96.9 us -> 93 us (0.960)
  Pallas kernels: 94.1 us -> 91.8 us
  local copies, waits for them, and re-layouts: 2.07 us -> 0 us
    pallas_call x1, Pallas kernels: 94.1 us -> 90.9 us  [local(): pl.pallas_call(kernel, out_shape=(jax.ShapeDtypeStruct((RANK, N), F32), j...]
    unnamed x3 -> x0, local copies, waits for them, and re-layouts: 2.07 us -> none
where the time goes in v3:
time: 93 us; the launch traced here: 92.6 us
  Pallas kernels  91.8 us (99%)
    pallas_call x1, Pallas kernels, local(): pl.pallas_call(kernel, out_shape=(jax.ShapeDtypeStruct((RANK, N), F32), j...  90.9 us

profile of v3, /device:TPU:0, one launch (start us, length us, event | category | flops | bytes accessed | tf_op | source)
XLA Modules:
  0.0 92.6 jit_solution(13895031658960092790)
XLA Ops:
  0.6 90.9 %shard_map.58 = (f32[96,672]{1,0:T(8,128)S(1)}, f32[96,672]{1,0:T(8,128)S(1)}, f32[192,96]{1,0:T(8,128)S(1)}) custom-call(f32[1344,672]{1,0:T(8,128)} %bitcast.6, f32[96,672]{1,0:T(8,128)} %bitcast.7, f32[96,672]{1,0:T(8,128)} %bitcast.8), custom_call_target="tpu_custom_call" | custom-call | tf_op jit(solution)/shard_map/pallas_call | solution.py:448
  91.6 0.9 shard_map.59

commit v4 on v3

--- a/solution.py
+++ b/solution.py
@@ -63,9 +63,6 @@
     core = lax.rem(slab, 2)
     chip = grp * 16 + slab // 2
 
-    def peer(t):
-        return (t // 16, lax.rem(t, 16) * 2 + core)
-
     zs = [grp] + [lax.rem(grp + d, 4) for d in range(1, 4)]
     ys = [lax.rem(slab // 8 + d, 4) * 4 for d in range(4)]
     xs = [lax.rem(slab // 2 + d, 4) for d in range(4)]
@@ -81,21 +78,16 @@
             (start_one, start_two)[i], starts.at[i], load_sem.at[CHUNKS + i]
         )
 
-    barrier = pltpu.get_barrier_semaphore()
-
-    def greet(k, carry):
-        pl.semaphore_signal(
-            barrier, inc=1, device_id=peer(lax.rem(chip + k, CHIPS)), device_id_type=MESH
-        )
-        return carry
-
-    lax.fori_loop(1, CHIPS, greet, 0)
-    pl.semaphore_signal(barrier, inc=1, device_id=twin, device_id_type=MESH)
-
     load_start(0).start()
     for c in range(CHUNKS):
         load(c).start()
     load_start(1).start()
+
+    barrier = pltpu.get_barrier_semaphore()
+    for dz, dy, dx in FAR_FIRST:
+        other = (zs[dz], (ys[dy] + xs[dx]) * 2 + core)
+        pl.semaphore_signal(barrier, inc=1, device_id=other, device_id_type=MESH)
+    pl.semaphore_signal(barrier, inc=1, device_id=twin, device_id_type=MESH)
 
     def set_block(x, rows):
         exact[0:rows, :] = x[0:rows]
@@ -109,20 +101,15 @@
         set_block(wide[...].T, NP)
 
     def prepare(c):
-        load(c).wait()
         rows = pl.ds(c * CHUNK, CHUNK)
         x = staged[c, :, 0:640]
-        squares = jnp.sum((x * x).reshape(CHUNK // 8, 8, 640), axis=0)
-        for k in range(5):
-            packed[0, 63] += squares[:, k * LANES : (k + 1) * LANES]
-        h, l = split(x)
-        high[rows, 0:640] = h
-        low[rows, 0:640] = l
-        x = staged[c, :, 640:N]
-        packed[0, 63, :, 0 : N - 640] += jnp.sum((x * x).reshape(CHUNK // 8, 8, N - 640), axis=0)
-        h, l = split(x)
-        high[rows, 640:N] = h
-        low[rows, 640:N] = l
+        y = staged[c, :, 640:N]
+        high[rows, 0:640], low[rows, 0:640] = split(x)
+        high[rows, 640:N], low[rows, 640:N] = split(y)
+        x = jnp.sum((x * x).reshape(CHUNK // 8, 8, 640), axis=0)
+        y = jnp.sum((y * y).reshape(CHUNK // 8, 8, N - 640), axis=0)
+        y = jnp.concatenate([y, jnp.zeros((8, NP - N), F32)], axis=1)
+        return sum((x[:, k * LANES : (k + 1) * LANES] for k in range(5)), y)
 
     def project(c):
         rows = pl.ds(c * CHUNK, CHUNK)
@@ -133,7 +120,8 @@
         total = None
         for c in range(CHUNKS):
             rows = pl.ds(c * CHUNK, CHUNK)
-            prepare(c)
+            squares = prepare(c)
+            packed[0, 63] = squares if c == 0 else packed[0, 63] + squares
             yh, yl = split(project(c))
             y = jnp.concatenate([yh, yl], axis=1)
             part = tops(dot(y, high[rows, :], NT) + dot(y, low[rows, :], NT))
@@ -159,7 +147,7 @@
 
     def product_gram():
         v = block[...]
-        width[...] = halves(dot(ghigh[...], v, NN) + dot(glow[...], v, NN))
+        width[0:N, :] = halves(dot(ghigh[0:N, :], v, NN) + dot(glow[0:N, :], v, NN))
 
     def product_two():
         v = block[0:N, :]
@@ -192,15 +180,17 @@
             x = gathered[r, b * tiles : (b + 1) * tiles].reshape(FOLD, LANES) * scale
             x0 = jnp.where(lanes < RANK, x, 0.0)
             exact[b * FOLD : (b + 1) * FOLD, :] = x0
-            h, l = split(x0)
-            block[b * FOLD : (b + 1) * FOLD, :LANES] = h
-            block[b * FOLD : (b + 1) * FOLD, LANES:] = l
+            if r % 2 == 0:
+                h, l = split(x0)
+                block[b * FOLD : (b + 1) * FOLD, :LANES] = h
+                block[b * FOLD : (b + 1) * FOLD, LANES:] = l
             moved = pltpu.roll(x, 32 * b + 32, 1)
             tail = jnp.where((lanes >= 32 * b) & (lanes < 32 * b + 32), moved, tail)
         exact[3 * FOLD : N, :] = tail
-        h, l = split(tail)
-        block[3 * FOLD : N, :LANES] = h
-        block[3 * FOLD : N, LANES:] = l
+        if r % 2 == 0:
+            h, l = split(tail)
+            block[3 * FOLD : N, :LANES] = h
+            block[3 * FOLD : N, LANES:] = l
 
     def send_all(r, src, dst, stage):
         for dz, dy, dx in FAR_FIRST:
@@ -227,10 +217,10 @@
         if first is not None:
             first()
         bytes_of(summed, r, recv_sem.at[r, 0]).wait()
-        total = summed[r, 0]
-        for t in range(1, CHIPS):
-            total = total + summed[r, t]
-        pair[r, pl.ds(core, 1)] = total[None]
+        parts = [summed[r, t] for t in range(CHIPS)]
+        while len(parts) > 1:
+            parts = [a + b for a, b in zip(parts[0::2], parts[1::2])]
+        pair[r, pl.ds(core, 1)] = parts[0][None]
         twin_copy = pltpu.make_async_remote_copy(
             src_ref=pair.at[r, core],
             dst_ref=pair.at[r, core],
@@ -240,14 +230,12 @@
             device_id_type=MESH,
         )
         twin_copy.start()
-        twin_copy.wait()
+        twin_copy.wait_recv()
         gathered[r, pl.ds(chip, 1)] = (pair[r, 0] + pair[r, 1])[None]
         send_all(r, gathered, gathered, 2)
         if last is not None:
             last()
         bytes_of(gathered, r, recv_sem.at[r, 2]).wait()
-        bytes_of(packed, r, send_sem.at[r, 0]).wait()
-        bytes_of(gathered, r, send_sem.at[r, 2]).wait()
         unpack(r)
 
     def cross_of():
@@ -311,7 +299,6 @@
     def factor_end():
         panels(4, 8)
         panels(8, 12)
-        stack()
 
     def basis():
         return lax.dot_general(
@@ -322,12 +309,14 @@
     def apply(rows):
         return lax.dot_general(exact[rows, :], inverse[...], TN, precision=lax.Precision.HIGHEST, preferred_element_type=F32)
 
-    packed[:, 63] = jnp.zeros((4, 8, LANES), F32)
+    packed[1:, 63] = jnp.zeros((3, 8, LANES), F32)
     high[:, 640:NP] = jnp.zeros((high.shape[0], LANES), BF16)
     low[:, 640:NP] = jnp.zeros((low.shape[0], LANES), BF16)
     inverse[...] = jnp.zeros_like(inverse)
     wide[...] = jnp.zeros_like(wide)
     pad_start(0)
+    for c in range(CHUNKS):
+        load(c).wait()
     product_one()
     reduce_block(0, gram_high, gram_low)
     product_gram()
@@ -383,6 +372,7 @@
         given[c, pl.ds(grp, 1)] = mode[c, pl.ds(grp, 1)]
     factor_start()
     factor_end()
+    stack()
     out_one[...] = basis()
     width[N:NP, :] = jnp.zeros((NP - N, LANES), F32)
     pad_start(1)
@@ -423,13 +413,16 @@
     three(core_in, swap_recv.at[CHUNKS]).wait()
     for g in range(GRP):
         unfold(core_in.at[g], 0, CORE_BODY, CORE_TAIL)
+        x = jnp.concatenate([line[0:RANK, :], line[RANK : 2 * RANK, :]], axis=1)
+        y = jnp.dot(mine, x, precision=lax.Precision.HIGHEST)
         for m in range(2):
-            x = line[m * RANK : (m + 1) * RANK, :]
-            out_core[pl.ds(2 * g + m, 24, stride=COLS), :] = jnp.dot(
-                mine, x, precision=lax.Precision.HIGHEST
-            )[:, :RANK]
+            out_core[pl.ds(2 * g + m, 24, stride=COLS), :] = y[:, m * LANES : m * LANES + RANK]
     for k in range(1, GRP):
         pltpu.make_async_copy(core_out, core_out, swap_send.at[CHUNKS]).wait()
+    for r in range(4):
+        bytes_of(packed, r, send_sem.at[r, 0]).wait()
+        pltpu.make_async_copy(pair.at[r, 0], pair.at[r, 0], send_sem.at[r, 1]).wait()
+        bytes_of(gathered, r, send_sem.at[r, 2]).wait()
 
 
 def finish(one, two, core, out_one, out_two, out_core, sems):

time: 93 us -> 90 us (0.968)
  Pallas kernels: 91.8 us -> 88.6 us
    pallas_call x1, Pallas kernels: 90.9 us -> 87.8 us  [local(): pl.pallas_call(kernel, out_shape=(jax.ShapeDtypeStruct((RANK, N), F32), j...]
where the time goes in v4:
time: 90 us; the launch traced here: 89.4 us
  Pallas kernels  88.6 us (98%)
    pallas_call x1, Pallas kernels, local(): pl.pallas_call(kernel, out_shape=(jax.ShapeDtypeStruct((RANK, N), F32), j...  87.8 us

profile of v4, /device:TPU:0, one launch (start us, length us, event | category | flops | bytes accessed | tf_op | source)
XLA Modules:
  0.0 89.4 jit_solution(1109595764030704246)
XLA Ops:
  0.6 87.8 %shard_map.58 = (f32[96,672]{1,0:T(8,128)S(1)}, f32[96,672]{1,0:T(8,128)S(1)}, f32[192,96]{1,0:T(8,128)S(1)}) custom-call(f32[1344,672]{1,0:T(8,128)} %bitcast.6, f32[96,672]{1,0:T(8,128)} %bitcast.7, f32[96,672]{1,0:T(8,128)} %bitcast.8), custom_call_target="tpu_custom_call" | custom-call | tf_op jit(solution)/shard_map/pallas_call | solution.py:441
  88.4 0.9 shard_map.59

commit v5 on v4

--- a/solution.py
+++ b/solution.py
@@ -53,10 +53,10 @@
 
 def kernel(
     tensor, start_one, start_two, out_one, out_two, out_core,
-    staged, starts, wide, gram, cross_part, ghigh, glow, high, low, block, exact, width, rhigh, rlow, rtilde, line, mode, given,
+    staged, starts, wide, gram, gram_in, cross_part, ghigh, glow, high, low, block, exact, width, rhigh, rlow, rtilde, line, mode, given,
     packed, summed, pair, gathered, core_out, core_in,
     unit, upper, lower, inverse, stacked,
-    load_sem, send_sem, recv_sem, swap_send, swap_recv,
+    load_sem, send_sem, recv_sem, swap_send, swap_recv, gram_send, gram_recv,
 ):
     grp = lax.axis_index("grp")
     slab = lax.axis_index("slab")
@@ -128,19 +128,42 @@
             total = part if total is None else total + part
         width[...] = total.T
 
-    def gram_high():
+    def gram_block(n, i, right, start):
+        rows = slice(i * 256, (i + 1) * 256)
+        if n == 0:
+            return dot(high[:, rows], right[:, start:], NT)
+        return dot(rhigh[rows, :], right[start:, :], TN)
+
+    def gram_copy(n, i):
+        part = (n, pl.ds(i * 256, 256), pl.ds(i * 256, NP - i * 256))
+        return pltpu.make_async_remote_copy(
+            src_ref=gram.at[part],
+            dst_ref=gram_in.at[part],
+            send_sem=gram_send.at[n, i],
+            recv_sem=gram_recv.at[n, i],
+            device_id=twin,
+            device_id_type=MESH,
+        )
+
+    def gram_start(n):
         for i in range(3):
-            a = high[:, i * 256 : (i + 1) * 256]
-            gram[i * 256 : (i + 1) * 256, i * 256 :] = dot(a, high[:, i * 256 :], NT)
-
-    def gram_low():
+            rows = slice(i * 256, (i + 1) * 256)
+            gram[n, rows, i * 256 :] = gram_block(n, i, (high, rhigh)[n], i * 256)
         for i in range(3):
-            a = high[:, i * 256 : (i + 1) * 256]
-            cross_part[i * 256 : (i + 1) * 256, :] = dot(a, low[...], NT)
+            rows = slice(i * 256, (i + 1) * 256)
+            cross_part[rows, :] = gram_block(n, i, (low, rlow)[n], 0)
         for i in range(3):
             for j in range(i, 3):
                 a, b = slice(i * 256, (i + 1) * 256), slice(j * 256, (j + 1) * 256)
-                x = gram[a, b] + cross_part[a, b] + cross_part[b, a].T
+                gram[n, a, b] = gram[n, a, b] + cross_part[a, b] + cross_part[b, a].T
+            gram_copy(n, i).start()
+
+    def gram_pair(n):
+        for i in range(3):
+            gram_copy(n, i).wait_recv()
+            for j in range(i, 3):
+                a, b = slice(i * 256, (i + 1) * 256), slice(j * 256, (j + 1) * 256)
+                x = gram[n, a, b] + gram_in[n, a, b]
                 ghigh[a, b], glow[a, b] = split(x)
                 if i != j:
                     ghigh[b, a], glow[b, a] = split(x.T)
@@ -151,10 +174,10 @@
 
     def product_two():
         v = block[0:N, :]
-        z = halves(dot(rhigh[...], v, NT) + dot(rlow[...], v, NT))
+        z = halves(dot(rhigh[0:N, :], v, NT) + dot(rlow[0:N, :], v, NT))
         zh, zl = split(z)
         zz = jnp.concatenate([zh, zl], axis=1)
-        width[0:N, :] = halves(dot(rhigh[...], zz, NN) + dot(rlow[...], zz, NN))
+        width[0:N, :] = halves(dot(rhigh[0:N, :], zz, NN) + dot(rlow[0:N, :], zz, NN))
 
     def pack(r):
         tail = width[3 * FOLD : N, :]
@@ -220,18 +243,21 @@
         parts = [summed[r, t] for t in range(CHIPS)]
         while len(parts) > 1:
             parts = [a + b for a, b in zip(parts[0::2], parts[1::2])]
-        pair[r, pl.ds(core, 1)] = parts[0][None]
-        twin_copy = pltpu.make_async_remote_copy(
-            src_ref=pair.at[r, core],
-            dst_ref=pair.at[r, core],
-            send_sem=send_sem.at[r, 1],
-            recv_sem=recv_sem.at[r, 1],
-            device_id=twin,
-            device_id_type=MESH,
-        )
-        twin_copy.start()
-        twin_copy.wait_recv()
-        gathered[r, pl.ds(chip, 1)] = (pair[r, 0] + pair[r, 1])[None]
+        total = parts[0]
+        if r % 2 == 0:
+            pair[r, pl.ds(core, 1)] = total[None]
+            twin_copy = pltpu.make_async_remote_copy(
+                src_ref=pair.at[r, core],
+                dst_ref=pair.at[r, core],
+                send_sem=send_sem.at[r, 1],
+                recv_sem=recv_sem.at[r, 1],
+                device_id=twin,
+                device_id_type=MESH,
+            )
+            twin_copy.start()
+            twin_copy.wait_recv()
+            total = pair[r, 0] + pair[r, 1]
+        gathered[r, pl.ds(chip, 1)] = total[None]
         send_all(r, gathered, gathered, 2)
         if last is not None:
             last()
@@ -313,12 +339,14 @@
     high[:, 640:NP] = jnp.zeros((high.shape[0], LANES), BF16)
     low[:, 640:NP] = jnp.zeros((low.shape[0], LANES), BF16)
     inverse[...] = jnp.zeros_like(inverse)
+    rhigh[N:NP, :] = jnp.zeros((NP - N, 2 * LANES), BF16)
+    rlow[N:NP, :] = jnp.zeros((NP - N, 2 * LANES), BF16)
     wide[...] = jnp.zeros_like(wide)
     pad_start(0)
     for c in range(CHUNKS):
         load(c).wait()
     product_one()
-    reduce_block(0, gram_high, gram_low)
+    reduce_block(0, lambda: gram_start(0), lambda: gram_pair(0))
     product_gram()
     reduce_block(1, factor_start, factor_end)
     set_block(apply(slice(0, N)), N)
@@ -394,12 +422,12 @@
         three(mode.at[c], swap_send.at[c]).wait()
 
     product_two()
-    reduce_block(2)
-    product_two()
+    reduce_block(2, lambda: gram_start(1), lambda: gram_pair(1))
+    product_gram()
     reduce_block(3, factor_start, factor_end)
     set_block(apply(slice(0, N)), N)
     v = block[0:N, :]
-    partial = tops(dot(v, rhigh[...], NT) + dot(v, rlow[...], NT))
+    partial = tops(dot(v, rhigh[0:N, :], NT) + dot(v, rlow[0:N, :], NT))
     for m in range(2):
         line[m * RANK : (m + 1) * RANK, :] = partial[0:RANK, m * LANES : (m + 1) * LANES]
     fold(core_out, CORE_BODY, CORE_TAIL)
@@ -419,9 +447,13 @@
             out_core[pl.ds(2 * g + m, 24, stride=COLS), :] = y[:, m * LANES : m * LANES + RANK]
     for k in range(1, GRP):
         pltpu.make_async_copy(core_out, core_out, swap_send.at[CHUNKS]).wait()
+    for i in range(3):
+        gram_copy(0, i).wait_send()
+        gram_copy(1, i).wait_send()
     for r in range(4):
         bytes_of(packed, r, send_sem.at[r, 0]).wait()
-        pltpu.make_async_copy(pair.at[r, 0], pair.at[r, 0], send_sem.at[r, 1]).wait()
+        if r % 2 == 0:
+            pltpu.make_async_copy(pair.at[r, 0], pair.at[r, 0], send_sem.at[r, 1]).wait()
         bytes_of(gathered, r, send_sem.at[r, 2]).wait()
 
 
@@ -451,7 +483,8 @@
             pltpu.VMEM((CHUNKS, CHUNK, N), F32),
             pltpu.VMEM((2, RANK, N), F32),
             pltpu.VMEM((LANES, NP), F32),
-            pltpu.VMEM((NP, NP), F32),
+            pltpu.VMEM((2, NP, NP), F32),
+            pltpu.VMEM((2, NP, NP), F32),
             pltpu.VMEM((NP, NP), F32),
             pltpu.VMEM((NP, NP), BF16),
             pltpu.VMEM((NP, NP), BF16),
@@ -460,8 +493,8 @@
             pltpu.VMEM((NP, 2 * LANES), BF16),
             pltpu.VMEM((NP, LANES), F32),
             pltpu.VMEM((NP, LANES), F32),
-            pltpu.VMEM((N, 2 * LANES), BF16),
-            pltpu.VMEM((N, 2 * LANES), BF16),
+            pltpu.VMEM((NP, 2 * LANES), BF16),
+            pltpu.VMEM((NP, 2 * LANES), BF16),
             pltpu.VMEM((rows, LANES), F32),
             pltpu.VMEM((CHUNK, LANES), F32),
             pltpu.VMEM((CHUNKS, GRP, BODY, LANES), F32),
@@ -482,6 +515,8 @@
             pltpu.SemaphoreType.DMA((4, 3)),
             pltpu.SemaphoreType.DMA((CHUNKS + 1,)),
             pltpu.SemaphoreType.DMA((CHUNKS + 1,)),
+            pltpu.SemaphoreType.DMA((2, 3)),
+            pltpu.SemaphoreType.DMA((2, 3)),
         ],
         compiler_params=pltpu.CompilerParams(
             collective_id=0, has_side_effects=True, vmem_limit_bytes=48 << 20

time: 90 us -> 86.5 us (0.961)
  Pallas kernels: 88.6 us -> 85.6 us
    pallas_call x1, Pallas kernels: 87.8 us -> 84.8 us  [local(): pl.pallas_call(kernel, out_shape=(jax.ShapeDtypeStruct((RANK, N), F32), j...]
where the time goes in v5:
time: 86.5 us; the launch traced here: 86.4 us
  Pallas kernels  85.6 us (99%)
    pallas_call x1, Pallas kernels, local(): pl.pallas_call(kernel, out_shape=(jax.ShapeDtypeStruct((RANK, N), F32), j...  84.8 us

profile of v5, /device:TPU:0, one launch (start us, length us, event | category | flops | bytes accessed | tf_op | source)
XLA Modules:
  0.0 86.4 jit_solution(1593723620353633453)
XLA Ops:
  0.6 84.8 %shard_map.58 = (f32[96,672]{1,0:T(8,128)S(1)}, f32[96,672]{1,0:T(8,128)S(1)}, f32[192,96]{1,0:T(8,128)S(1)}) custom-call(f32[1344,672]{1,0:T(8,128)} %bitcast.6, f32[96,672]{1,0:T(8,128)} %bitcast.7, f32[96,672]{1,0:T(8,128)} %bitcast.8), custom_call_target="tpu_custom_call" | custom-call | tf_op jit(solution)/shard_map/pallas_call | solution.py:473
  85.4 0.9 shard_map.59

commit v6 on v5

--- a/solution.py
+++ b/solution.py
@@ -53,7 +53,7 @@
 
 def kernel(
     tensor, start_one, start_two, out_one, out_two, out_core,
-    staged, starts, wide, gram, gram_in, cross_part, ghigh, glow, high, low, block, exact, width, rhigh, rlow, rtilde, line, mode, given,
+    staged, starts, wide, second, gram, gram_in, cross_part, ghigh, glow, high, low, block, exact, width, rhigh, rlow, rtilde, line, mode, given,
     packed, summed, pair, gathered, core_out, core_in,
     unit, upper, lower, inverse, stacked,
     load_sem, send_sem, recv_sem, swap_send, swap_recv, gram_send, gram_recv,
@@ -78,27 +78,27 @@
             (start_one, start_two)[i], starts.at[i], load_sem.at[CHUNKS + i]
         )
 
-    load_start(0).start()
-    for c in range(CHUNKS):
-        load(c).start()
-    load_start(1).start()
-
     barrier = pltpu.get_barrier_semaphore()
     for dz, dy, dx in FAR_FIRST:
         other = (zs[dz], (ys[dy] + xs[dx]) * 2 + core)
         pl.semaphore_signal(barrier, inc=1, device_id=other, device_id_type=MESH)
     pl.semaphore_signal(barrier, inc=1, device_id=twin, device_id_type=MESH)
 
+    load_start(0).start()
+    for c in range(CHUNKS):
+        load(c).start()
+    load_start(1).start()
+
     def set_block(x, rows):
         exact[0:rows, :] = x[0:rows]
         h, l = split(x)
         block[0:rows, :LANES] = h
         block[0:rows, LANES:] = l
 
-    def pad_start(i):
+    def pad_start(i, target):
         load_start(i).wait()
         wide[0:RANK, 0:N] = starts[i]
-        set_block(wide[...].T, NP)
+        target[:, :LANES], target[:, LANES:] = split(wide[...].T)
 
     def prepare(c):
         rows = pl.ds(c * CHUNK, CHUNK)
@@ -173,7 +173,7 @@
         width[0:N, :] = halves(dot(ghigh[0:N, :], v, NN) + dot(glow[0:N, :], v, NN))
 
     def product_two():
-        v = block[0:N, :]
+        v = second[0:N, :]
         z = halves(dot(rhigh[0:N, :], v, NT) + dot(rlow[0:N, :], v, NT))
         zh, zl = split(z)
         zz = jnp.concatenate([zh, zl], axis=1)
@@ -335,6 +335,14 @@
     def apply(rows):
         return lax.dot_general(exact[rows, :], inverse[...], TN, precision=lax.Precision.HIGHEST, preferred_element_type=F32)
 
+    def first_window():
+        factor_start()
+        pad_start(1, second)
+
+    def third_window():
+        gram_pair(1)
+        out_one[...] = basis()
+
     packed[1:, 63] = jnp.zeros((3, 8, LANES), F32)
     high[:, 640:NP] = jnp.zeros((high.shape[0], LANES), BF16)
     low[:, 640:NP] = jnp.zeros((low.shape[0], LANES), BF16)
@@ -342,13 +350,13 @@
     rhigh[N:NP, :] = jnp.zeros((NP - N, 2 * LANES), BF16)
     rlow[N:NP, :] = jnp.zeros((NP - N, 2 * LANES), BF16)
     wide[...] = jnp.zeros_like(wide)
-    pad_start(0)
+    pad_start(0, block)
     for c in range(CHUNKS):
         load(c).wait()
     product_one()
     reduce_block(0, lambda: gram_start(0), lambda: gram_pair(0))
     product_gram()
-    reduce_block(1, factor_start, factor_end)
+    reduce_block(1, first_window, factor_end)
     set_block(apply(slice(0, N)), N)
 
     def fold(target, body, tail):
@@ -401,9 +409,6 @@
     factor_start()
     factor_end()
     stack()
-    out_one[...] = basis()
-    width[N:NP, :] = jnp.zeros((NP - N, LANES), F32)
-    pad_start(1)
     f = stacked[...]
     for c in range(CHUNKS):
         three(given.at[c], swap_recv.at[c]).wait()
@@ -422,7 +427,7 @@
         three(mode.at[c], swap_send.at[c]).wait()
 
     product_two()
-    reduce_block(2, lambda: gram_start(1), lambda: gram_pair(1))
+    reduce_block(2, lambda: gram_start(1), third_window)
     product_gram()
     reduce_block(3, factor_start, factor_end)
     set_block(apply(slice(0, N)), N)
@@ -483,6 +488,7 @@
             pltpu.VMEM((CHUNKS, CHUNK, N), F32),
             pltpu.VMEM((2, RANK, N), F32),
             pltpu.VMEM((LANES, NP), F32),
+            pltpu.VMEM((NP, 2 * LANES), BF16),
             pltpu.VMEM((2, NP, NP), F32),
             pltpu.VMEM((2, NP, NP), F32),
             pltpu.VMEM((NP, NP), F32),

time: 86.5 us -> 86.1 us (level)
  no operation moved by 1% of the time
where the time goes in v6:
time: 86.1 us; the launch traced here: 86 us
  Pallas kernels  85.2 us (99%)
    pallas_call x1, Pallas kernels, local(): pl.pallas_call(kernel, out_shape=(jax.ShapeDtypeStruct((RANK, N), F32), j...  84.3 us

profile of v6, /device:TPU:0, one launch (start us, length us, event | category | flops | bytes accessed | tf_op | source)
XLA Modules:
  0.0 86.0 jit_solution(14357464813708341541)
XLA Ops:
  0.6 84.3 %shard_map.58 = (f32[96,672]{1,0:T(8,128)S(1)}, f32[96,672]{1,0:T(8,128)S(1)}, f32[192,96]{1,0:T(8,128)S(1)}) custom-call(f32[1344,672]{1,0:T(8,128)} %bitcast.6, f32[96,672]{1,0:T(8,128)} %bitcast.7, f32[96,672]{1,0:T(8,128)} %bitcast.8), custom_call_target="tpu_custom_call" | custom-call | tf_op jit(solution)/shard_map/pallas_call | solution.py:478
  85.0 0.9 %shard_map.59 = (f32[96,672]{1,0:T(8,128)}, f32[96,672]{1,0:T(8,128)}, f32[192,96]{1,0:T(8,128)}) custom-call(f32[96,672]{1,0:T(8,128)S(1)} %get-tuple-element.9.one, f32[96,672]{1,0:T(8,128)S(1)} %get-tuple-element.10.two, f32[192,96]{1,0:T(8,128)S(1)} %get-tuple-element.11.core), custom_call_target="tpu_custom_call" | custom-call | tf_op jit(solution)/shard_map/pallas_call | solution.py:535

commit v7 on v6

--- a/solution.py
+++ b/solution.py
@@ -333,7 +333,15 @@
         )
 
     def apply(rows):
-        return lax.dot_general(exact[rows, :], inverse[...], TN, precision=lax.Precision.HIGHEST, preferred_element_type=F32)
+        x = exact[rows, :]
+        high_x, mid_x = split(x)
+        low_x = (x - high_x.astype(F32) - mid_x.astype(F32)).astype(BF16)
+        f = inverse[...]
+        high_f, mid_f = split(f)
+        low_f = (f - high_f.astype(F32) - mid_f.astype(F32)).astype(BF16)
+        two = jnp.concatenate([high_f, mid_f], axis=0)
+        main = halves(dot(high_x, two, TN) + dot(mid_x, two, TN))
+        return main + (dot(high_x, low_f, TN) + dot(low_x, high_f, TN))
 
     def first_window():
         factor_start()

time: 86.1 us -> 85.8 us (level)
  no operation moved by 1% of the time
where the time goes in v7:
time: 85.8 us; the launch traced here: 85.7 us
  Pallas kernels  84.9 us (99%)
    pallas_call x1, Pallas kernels, local(): pl.pallas_call(kernel, out_shape=(jax.ShapeDtypeStruct((RANK, N), F32), j...  84 us

profile of v7, /device:TPU:0, one launch (start us, length us, event | category | flops | bytes accessed | tf_op | source)
XLA Modules:
  0.0 85.7 jit_solution(15337702398831015292)
XLA Ops:
  0.6 84.0 %shard_map.58 = (f32[96,672]{1,0:T(8,128)S(1)}, f32[96,672]{1,0:T(8,128)S(1)}, f32[192,96]{1,0:T(8,128)S(1)}) custom-call(f32[1344,672]{1,0:T(8,128)} %bitcast.6, f32[96,672]{1,0:T(8,128)} %bitcast.7, f32[96,672]{1,0:T(8,128)} %bitcast.8), custom_call_target="tpu_custom_call" | custom-call | tf_op jit(solution)/shard_map/pallas_call | solution.py:486
  84.7 0.9 %shard_map.59 = (f32[96,672]{1,0:T(8,128)}, f32[96,672]{1,0:T(8,128)}, f32[192,96]{1,0:T(8,128)}) custom-call(f32[96,672]{1,0:T(8,128)S(1)} %get-tuple-element.9.one, f32[96,672]{1,0:T(8,128)S(1)} %get-tuple-element.10.two, f32[192,96]{1,0:T(8,128)S(1)} %get-tuple-element.11.core), custom_call_target="tpu_custom_call" | custom-call | tf_op jit(solution)/shard_map/pallas_call | solution.py:543
